TPU v7x, 512 devices: a whole 4x4x16 slice. The times are simulated.
512 devices in a mesh: query: 4 (over x), corpus: 16 (over z), cent: 8 (over y, core).
Axes of the slice: x: 4, y: 4, z: 16, core: 2. Of those that a mesh axis runs over, the one named last changes fastest.
Arguments:
- request_term_embeds: bfloat16 [64, 32, 128], P('query'), may hold values from -6 to 6
- cluster_means: bfloat16 [65536, 128], P(('corpus', 'cent')), may hold values from -0.5 to 0.5
- cluster_shard_number: int32 [8192, 64, 1], P(('corpus', 'cent')), may hold values from 0 to 127; in each aligned block of 4096 rows (0 to 4095, 4096 to 8191, ..., all dimensions but the last counted through in order) at most 64 rows name the same one
- cluster_entry_within: int32 [8192, 64], P(('corpus', 'cent')), may hold values from 0 to 511
- quantized_error_words: int32 [8192, 1024], P(('corpus', 'cent')), may hold values from 0 to 65535
- quantized_error_amounts: float32 [4], replicated, may hold values from -0.2 to 0.2
- keeper_document_position: int32 [64, 128, 16], P('query', ('corpus', 'cent')), may hold values from 0 to 63, as said below
- active_keeper_tally: int32 [64, 128], P('query', ('corpus', 'cent')), may hold values from 2 to 16, as said below
Outputs:
- approx_scores: float32 [64, 128, 16], P('query', ('corpus', 'cent'))
- exact_scores: float32 [64, 128, 16], P('query', ('corpus', 'cent'))
- best_scores: float32 [64, 8], P('query')
Inputs may be any that keep to these rules, and one draw needn't show every extreme that they name: `cluster_shard_number`: among the 4096 tokens of the passages of one device (aligned blocks of rows), no block value is named by more than 64 tokens; some value is named by exactly 64. `keeper_document_position`: the 16 slots of one query on one shard name different passages. `active_keeper_tally`: every query has 16 live slots on some passage shard.
All inputs are finite; a program needn't handle non-finite values.
Results may differ from a plain program's by a relative error of at most 0.00033.
Values may be sent and summed in bfloat16 or wider, within the bound.
A program may use at most 64 MiB of HBM per device.

v0:
```python
import jax
import jax.numpy as jnp
from jax import lax
from jax.sharding import PartitionSpec as P

TOPK = 8


eps_norm = 1e-06
minimum_similarity = -1e30


def merged(value, axis, join):
    pieces = lax.all_gather(value, axis)
    head = pieces[0]
    tail = pieces[1:]
    subtotal, _ = lax.scan(lambda subtotal, section: (join(subtotal, section), None), head, tail)
    return subtotal


def unpack_residual(packed_words, quantized_error_amounts):
    shifts = 2 * jnp.arange(8, dtype=jnp.int32)
    codes = jnp.bitwise_and(jnp.right_shift(packed_words[..., None], shifts), 3)
    codes = codes.reshape(packed_words.shape[:-1] + (packed_words.shape[-1] * 8,))
    residual = jnp.zeros(codes.shape, jnp.float32)
    for level in range(4):
        residual = residual + jnp.where(
            codes == level, quantized_error_amounts[level], jnp.float32(0.0)
        )
    return residual


def normalize_rows(values):
    values = values.astype(jnp.float32)
    return values * lax.rsqrt(jnp.sum(values * values, axis=-1, keepdims=True) + eps_norm)


def one_hot_rows(local_ids, table):
    id_count = local_ids.shape[0]
    table_size = table.shape[0]
    tile_width = 128
    offsets = jnp.arange(tile_width, dtype=jnp.int32)

    def step(tile_index, running):
        first_row = tile_index * tile_width
        sub_table = lax.dynamic_slice_in_dim(table, first_row, tile_width, 0)
        matches = (local_ids[:, None] == first_row + offsets[None, :]).astype(jnp.bfloat16)
        return running + jnp.dot(matches, sub_table, preferred_element_type=jnp.bfloat16)

    initial = jnp.zeros((id_count, table.shape[1]), jnp.bfloat16)
    return lax.fori_loop(0, table_size // tile_width, step, initial)


def maxsim_flat(request_embeds, document_embeds):
    keeper_seat_total, document_terms, embedding_width = document_embeds.shape
    flattened_documents = document_embeds.reshape(
        keeper_seat_total * document_terms, embedding_width
    )
    similarity_matrix = jnp.einsum(
        "td,nd->tn", request_embeds, flattened_documents, preferred_element_type=jnp.float32
    )
    similarity_matrix = similarity_matrix.reshape(
        request_embeds.shape[0], keeper_seat_total, document_terms
    )
    return jnp.sum(jnp.max(similarity_matrix, axis=2), axis=0)


def local(
    request_term_embeds,
    cluster_means,
    cluster_shard_number,
    cluster_entry_within,
    quantized_error_words,
    quantized_error_amounts,
    keeper_document_position,
    active_keeper_tally,
):
    query_count, query_tokens, embedding_width = request_term_embeds.shape
    passage_count = cluster_shard_number.shape[0]
    document_terms = cluster_shard_number.shape[1]
    corpus_size = lax.axis_size("corpus")
    cent_size = lax.axis_size("cent")
    block_count = corpus_size * cent_size
    token_count = passage_count * document_terms
    capacity = 2 * token_count // block_count
    target_block = cluster_shard_number.reshape(token_count)
    wanted_rows = cluster_entry_within.reshape(token_count)
    block_iota = jnp.arange(block_count, dtype=jnp.int32)
    per_block = jnp.sum((target_block[:, None] == block_iota[None, :]).astype(jnp.int32), axis=0)
    block_first = jnp.cumsum(per_block) - per_block
    sorted_order = jnp.argsort(target_block, stable=True)
    sorted_rank = jnp.arange(token_count, dtype=jnp.int32) - block_first[target_block[sorted_order]]
    slot_rank = jnp.zeros((token_count,), jnp.int32).at[sorted_order].set(sorted_rank)
    requests = (
        jnp.zeros((block_count, capacity), jnp.int32).at[target_block, slot_rank].set(wanted_rows)
    )
    row_ids = lax.all_to_all(requests, ("corpus", "cent"), split_axis=0, concat_axis=0, tiled=True)
    found = one_hot_rows(row_ids.reshape(-1), cluster_means)
    looked_up = found.reshape(row_ids.shape + (embedding_width,))
    returned = lax.all_to_all(
        looked_up, ("corpus", "cent"), split_axis=0, concat_axis=0, tiled=True
    )
    centroid_rows = returned[target_block, slot_rank]
    request_embed_lines = normalize_rows(request_term_embeds).astype(jnp.bfloat16)
    words = quantized_error_words.reshape(passage_count, document_terms, embedding_width // 8)
    rows_by_passage = centroid_rows.reshape(passage_count, document_terms, embedding_width)
    chosen_documents = keeper_document_position[:, 0, :]

    def score_query(pair):
        request_embeds, local_ids = pair
        coarse_docs = rows_by_passage[local_ids]
        residual = unpack_residual(words[local_ids], quantized_error_amounts)
        fine_docs = normalize_rows(coarse_docs.astype(jnp.float32) + residual).astype(jnp.bfloat16)
        return (maxsim_flat(request_embeds, coarse_docs), maxsim_flat(request_embeds, fine_docs))

    coarse_slots, fine_slots = lax.map(score_query, (request_embed_lines, chosen_documents))
    keeper_seat_total = keeper_document_position.shape[2]
    seat_active_flag = (
        jnp.arange(keeper_seat_total, dtype=jnp.int32)[None, :] < active_keeper_tally[:, 0][:, None]
    )
    approx_scores = jnp.where(seat_active_flag, coarse_slots, jnp.float32(0.0))[:, None, :]
    exact_scores = jnp.where(seat_active_flag, fine_slots, jnp.float32(0.0))[:, None, :]
    padding = jnp.full((query_count, TOPK), minimum_similarity, jnp.float32)
    candidates = jnp.concatenate(
        [jnp.where(seat_active_flag, fine_slots, jnp.float32(minimum_similarity)), padding], axis=1
    )
    local_best = lax.top_k(candidates, TOPK)[0]

    def keep_best(first, second):
        return lax.top_k(jnp.concatenate([first, second], axis=1), first.shape[1])[0]

    best_scores = merged(local_best, ("corpus", "cent"), keep_best)
    return (approx_scores, exact_scores, best_scores)


def solution(mesh):
    return jax.shard_map(
        local,
        mesh=mesh,
        in_specs=(
            P("query", None, None),
            P(("corpus", "cent"), None),
            P(("corpus", "cent"), None, None),
            P(("corpus", "cent"), None),
            P(("corpus", "cent"), None),
            P(),
            P("query", ("corpus", "cent"), None),
            P("query", ("corpus", "cent")),
        ),
        out_specs=(
            P("query", ("corpus", "cent"), None),
            P("query", ("corpus", "cent"), None),
            P("query", None),
        ),
        check_vma=False,
    )
```

profile of v0, /device:TPU:1, one launch (start us, length us, event | category | flops | bytes accessed | tf_op | source)
XLA Modules:
  0.0 665.7 jit_solution(11826996376798566862)
XLA Ops:
  3.7 5.8 sort.21
  9.5 23.0 %gather_fusion.2 = s32[4096]{0:T(1024)S(1)} fusion(s32[4096]{0:T(1024)S(1)} %reshape.223, s32[4096]{0:T(1024)S(1)} %get-tuple-element.279), kind=kCustom, calls=%fused_computation.2 | custom fusion | bytes 49152 | tf_op jit(solution)/shard_map/gather | solution.py:92
  32.6 24.7 %gather_fusion.3 = s32[4096]{0:T(1024)S(1)} fusion(s32[128]{0:T(128)S(1)} %sub.6, s32[4096]{0:T(1024)S(1)} %broadcast_clamp_fusion), kind=kCustom, calls=%fused_computation.3 | custom fusion | bytes 49152 | tf_op jit(solution)/shard_map/gather | solution.py:92
  57.3 15.5 %scatter_custom_fusion = s32[4096]{0:T(1024)S(1)} fusion(s32[4096]{0:T(1024)S(1)} %get-tuple-element.280, s32[4096]{0:T(1024)S(1)} %iota_subtract_fusion, s32[]{:T(128)} %copy.101), kind=kCustom, calls=%fused_computation.68 | custom fusion | bytes 16388 | tf_op jit(solution)/shard_map/scatter | solution.py:93
  74.7 15.5 %scatter_custom_fusion.1 = s32[8192]{0:T(1024)S(1)} fusion(s32[4096]{0:T(1024)S(1)} %broadcast_select_fusion, s32[4096]{0:T(1024)S(1)} %reshape.283, s32[]{:T(128)} %copy.101), kind=kCustom, calls=%fused_computation.60 | custom fusion | bytes 32772
  90.9 20.6 %all-to-all-start = ((s32[128,1,64]{2,1,0:T(1,128)}), s32[128,1,64]{2,1,0:T(1,128)S(1)}, u32[]{:S(2)}, u32[]{:S(2)}) async-start(s32[128,1,64]{2,1,0:T(1,128)} %copy.61), calls=%async_computation | async-start | bytes 131072 | tf_op jit(solution)/shard_map/all_to_all | solution.py:97
  111.5 14.8 %all-to-all-done = s32[128,1,64]{2,1,0:T(1,128)S(1)} async-done(((s32[128,1,64]{2,1,0:T(1,128)}), s32[128,1,64]{2,1,0:T(1,128)S(1)}, u32[]{:S(2)}, u32[]{:S(2)}) %all-to-all-start) | async-done | bytes 32800 | tf_op jit(solution)/shard_map/all_to_all | solution.py:97
  127.0 28.3 %while.39 = (s32[]{:T(128)}, bf16[8192,128]{1,0:T(8,128)(2,1)S(1)}, s32[128,64]{1,0:T(8,128)}, bf16[512,128]{1,0:T(8,128)(2,1)}, s32[8192]{0:T(1024)S(1)}, /*index=5*/s32[]{:T(128)}, s32[]{:T(128)}, s32[]{:T(128)}, s32[]{:T(128)}) while((s32[]{:T(128)}, bf16[8192,128]{1,0:T(8,128)(2,1)S(1)}, s32[128,64]{1,0:T(8,128)}, ...), condition=%wide.wide.region_7.8_spmd.clone, body=%wide.wide.region_6.7_spmd.clone.sunk | while | flops 271581312 | bytes 4261021 | solution.py:51
  127.0 7.0 %convolution_add_fusion.3 = bf16[8192,128]{1,0:T(8,128)(2,1)S(1)} fusion(bf16[8192,128]{1,0:T(8,128)(2,1)S(1)} %get-tuple-element.419, s32[128]{0:T(128)S(1)} %iota_add_fusion.3, s32[8192]{0:T(1024)S(1)} %get-tuple-element.431, pred[]{:T(512)S(6)} %compare.49, bf16[512,128]{1,0:T(8,128)(2,1)} %get-tuple-element.430, s32[]{:T(128)S(6)} %select_n.200), kind=kOutput, calls=%fused_computation.39.clone.clone.1 | convolution fusion | flops 271581184 | bytes 4260357 | tf_op jit(solution)/shard_map/while/body/eval_jaxpr/dot_general | solution.py:48
  134.0 7.0 %convolution_add_fusion.3 = bf16[8192,128]{1,0:T(8,128)(2,1)S(1)} fusion(bf16[8192,128]{1,0:T(8,128)(2,1)S(1)} %get-tuple-element.419, s32[128]{0:T(128)S(1)} %iota_add_fusion.3, s32[8192]{0:T(1024)S(1)} %get-tuple-element.431, pred[]{:T(512)S(6)} %compare.49, bf16[512,128]{1,0:T(8,128)(2,1)} %get-tuple-element.430, s32[]{:T(128)S(6)} %select_n.200), kind=kOutput, calls=%fused_computation.39.clone.clone.1 | convolution fusion | flops 271581184 | bytes 4260357 | tf_op jit(solution)/shard_map/while/body/eval_jaxpr/dot_general | solution.py:48
  141.1 7.0 %convolution_add_fusion.3 = bf16[8192,128]{1,0:T(8,128)(2,1)S(1)} fusion(bf16[8192,128]{1,0:T(8,128)(2,1)S(1)} %get-tuple-element.419, s32[128]{0:T(128)S(1)} %iota_add_fusion.3, s32[8192]{0:T(1024)S(1)} %get-tuple-element.431, pred[]{:T(512)S(6)} %compare.49, bf16[512,128]{1,0:T(8,128)(2,1)} %get-tuple-element.430, s32[]{:T(128)S(6)} %select_n.200), kind=kOutput, calls=%fused_computation.39.clone.clone.1 | convolution fusion | flops 271581184 | bytes 4260357 | tf_op jit(solution)/shard_map/while/body/eval_jaxpr/dot_general | solution.py:48
  148.2 7.0 %convolution_add_fusion.3 = bf16[8192,128]{1,0:T(8,128)(2,1)S(1)} fusion(bf16[8192,128]{1,0:T(8,128)(2,1)S(1)} %get-tuple-element.419, s32[128]{0:T(128)S(1)} %iota_add_fusion.3, s32[8192]{0:T(1024)S(1)} %get-tuple-element.431, pred[]{:T(512)S(6)} %compare.49, bf16[512,128]{1,0:T(8,128)(2,1)} %get-tuple-element.430, s32[]{:T(128)S(6)} %select_n.200), kind=kOutput, calls=%fused_computation.39.clone.clone.1 | convolution fusion | flops 271581184 | bytes 4260357 | tf_op jit(solution)/shard_map/while/body/eval_jaxpr/dot_general | solution.py:48
  156.6 5.9 all-to-all-start.1
  163.4 95.1 %all-to-all-done.1 = bf16[128,64,128]{2,1,0:T(8,128)(2,1)S(1)} async-done(((bf16[128,64,128]{2,1,0:T(8,128)(2,1)}), bf16[128,64,128]{2,1,0:T(8,128)(2,1)S(1)}, u32[]{:S(2)}, u32[]{:S(2)}) %all-to-all-start.1) | async-done | bytes 2097184 | tf_op jit(solution)/shard_map/all_to_all | solution.py:100
  258.5 40.2 %gather_fusion.4 = bf16[4096,128]{1,0:T(8,128)(2,1)} fusion(bf16[128,64,128]{2,1,0:T(8,128)(2,1)S(1)} %all-to-all-done.1, s32[4096]{0:T(1024)S(1)} %bitcast.89), kind=kCustom, calls=%fused_computation.4 | custom fusion | bytes 2129920 | tf_op jit(solution)/shard_map/gather | solution.py:103
  298.7 184.6 %while.37 = (s32[]{:T(128)}, f32[16,16]{1,0:T(8,128)S(1)}, f32[16,16]{1,0:T(8,128)S(1)}, bf16[16,32,128]{2,1,0:T(8,128)(2,1)S(1)}, s32[16,16]{1,0:T(8,128)}, /*i...) while((s32[]{:T(128)}, f32[16,16]{1,0:T(8,128)S(1)}, ...), condition=%wide.region_14.15_spmd, body=%wide.region_8.14_spmd.sunk | while | flops 21169176 | bytes 5361097 | solution.py:116
  303.0 2.9 multiply_reduce_fusion.3
  306.1 3.4 convolution_reduce_fusion.5
  314.5 2.9 multiply_reduce_fusion.3
  317.7 3.4 convolution_reduce_fusion.5
  326.1 2.9 multiply_reduce_fusion.3
  329.2 3.4 convolution_reduce_fusion.5
  337.6 2.9 multiply_reduce_fusion.3
  340.7 3.4 convolution_reduce_fusion.5
  349.1 2.9 multiply_reduce_fusion.3
  352.3 3.4 convolution_reduce_fusion.5
  360.7 2.9 multiply_reduce_fusion.3
  363.8 3.4 convolution_reduce_fusion.5
  372.2 2.9 multiply_reduce_fusion.3
  375.4 3.4 convolution_reduce_fusion.5
  383.8 2.9 multiply_reduce_fusion.3
  386.9 3.4 convolution_reduce_fusion.5
  395.3 2.9 multiply_reduce_fusion.3
  398.4 3.4 convolution_reduce_fusion.5
  406.8 2.9 multiply_reduce_fusion.3
  410.0 3.4 convolution_reduce_fusion.5
  418.4 2.9 multiply_reduce_fusion.3
  421.5 3.4 convolution_reduce_fusion.5
  429.9 2.9 multiply_reduce_fusion.3
  433.1 3.4 convolution_reduce_fusion.5
  441.5 2.9 multiply_reduce_fusion.3
  444.6 3.4 convolution_reduce_fusion.5
  453.0 2.9 multiply_reduce_fusion.3
  456.1 3.4 convolution_reduce_fusion.5
  467.7 3.4 convolution_reduce_fusion.5
  479.2 3.4 convolution_reduce_fusion.5
  484.3 85.1 %all-gather.1 = f32[128,16,8]{1,2,0:T(8,128)S(1)} all-gather(f32[1,16,8]{1,2,0:T(8,128)S(1)} %slice_bitcast_fusion.1), channel_id=2, replica_groups=mesh['query'=4,'corpus'=16,'cent'=8] {'corpus','cent'}, dimensions={0}, use_global_device_ids=true | all-gather | bytes 66048 | tf_op jit(solution)/shard_map/all_gather | solution.py:14
  569.5 94.9 %while.38 = (s32[]{:T(128)}, f32[16,8]{0,1:T(8,128)S(1)}, f32[127,16,8]{1,2,0:T(8,128)S(1)}, s32[]{:T(128)}) while((s32[]{:T(128)}, f32[16,8]{0,1:T(8,128)S(1)}, f32[127,16,8]{1,2,0:T(8,128)S(1)}, s32[]{:T(128)}) %tuple.93), condition=%wide.region_18.19_spmd, body=%wide.region_16.18_spmd.sunk | while | flops 2306 | bytes 9273 | solution.py:17
  (976 shorter events, 193.8 us)
Async XLA Ops:
  32.6 40.8 %copy-start.6 = (s32[64,64,1]{1,2,0:T(1,128)S(1)}, s32[64,64,1]{1,2,0:T(1,128)}, u32[]{:S(2)}) copy-start(s32[64,64,1]{1,2,0:T(1,128)} %param.16) | copy-start | bytes 49156
  32.6 41.7 %copy-start.9 = (s32[2]{0:T(128)S(1)}, s32[2]{0:T(128)}, u32[]{:S(2)}) copy-start(s32[2]{0:T(128)} %constant.108) | copy-start | bytes 28
  32.6 41.8 %copy-start.8 = (s32[2]{0:T(128)S(1)}, s32[2]{0:T(128)}, u32[]{:S(2)}) copy-start(s32[2]{0:T(128)} %constant.111) | copy-start | bytes 28
  32.6 42.0 %copy-start.7 = (s32[64,64]{1,0:T(8,128)S(1)}, s32[64,64]{1,0:T(8,128)}, u32[]{:S(2)}) copy-start(s32[64,64]{1,0:T(8,128)} %param.17) | copy-start | bytes 49156
  90.9 35.4 %all-to-all-start = ((s32[128,1,64]{2,1,0:T(1,128)}), s32[128,1,64]{2,1,0:T(1,128)S(1)}, u32[]{:S(2)}, u32[]{:S(2)}) async-start(s32[128,1,64]{2,1,0:T(1,128)} %copy.61), calls=%async_computation | async-start | bytes 131072 | tf_op jit(solution)/shard_map/all_to_all | solution.py:97
  126.3 0.6 copy-start.3
  155.2 1.4 copy-start
  156.6 5.9 copy-start.2
  156.6 6.5 copy-start.1
  156.6 101.9 %all-to-all-start.1 = ((bf16[128,64,128]{2,1,0:T(8,128)(2,1)}), bf16[128,64,128]{2,1,0:T(8,128)(2,1)S(1)}, u32[]{:S(2)}, u32[]{:S(2)}) async-start(bf16[128,64,128]{2,1,0:T(8,128)(2,1)} %bitcast.91), calls=%async_computation.1 | async-start | bytes 4194304 | tf_op jit(solution)/shard_map/all_to_all | solution.py:100
  258.5 40.2 %copy-start.4 = (f32[4]{0:T(128)S(1)}, f32[4]{0:T(128)}, u32[]{:S(2)}) copy-start(f32[4]{0:T(128)} %param.19) | copy-start | bytes 52
  298.7 184.8 %copy-start.10 = (s32[16,1]{0,1:T(1,128)S(1)}, s32[16,1]{0,1:T(1,128)}, u32[]{:S(2)}) copy-start(s32[16,1]{0,1:T(1,128)} %param.21) | copy-start | bytes 196
  664.4 1.3 copy-start.5
where the time goes:
time: 669 us; the launch traced here: 666 us
  local copies, waits for them, and re-layouts  188 us (28%)
  other arithmetic  164 us (25%)
  waiting for transfers between devices  110 us (16%)
  matrix products  88.7 us (13%)
  blocking collectives  85.1 us (13%)
  starting transfers between devices  26.4 us (4%)
    all_to_all x1, waiting for transfers between devices, local(): lax.all_to_all(looked_up, ('corpus', 'cent'), split_axis=0, concat_axis=0...  95.1 us
    top_k x127, other arithmetic, keep_best(): lax.top_k(jnp.concatenate([first, second], axis=1), first.shape[1])[0]  92 us
    all_gather x1, blocking collectives, merged(): pieces = lax.all_gather(value, axis)  85.1 us
    dot_general x32, matrix products, maxsim_flat(): jnp.einsum('td,nd->tn', request_embeds, flattened_documents, preferred_el...  60.6 us
    reduce_sum x17, other arithmetic, normalize_rows(): jnp.sum(values * values, axis=-1, keepdims=True) + eps_norm  46.4 us
    gather x1, local copies, waits for them, and re-layouts, local(): centroid_rows = returned[target_block, slot_rank]  40.2 us
    gather x16, local copies, waits for them, and re-layouts, score_query(): coarse_docs = rows_by_passage[local_ids]  29.1 us
    dot_general x4, matrix products, step(): jnp.dot(matches, sub_table, preferred_element_type=jnp.bfloat16)  28.1 us
  transfers between devices with their start and end apart: 2, of which 2 were waited for; matrix products, arithmetic and copies ran while one was open for 0% of the time, Pallas kernels for 0%

commit v1 on v0

v1 whole, which is shorter than its diff:
```python
import functools

import jax
import jax.numpy as jnp
from jax import lax
from jax.experimental import pallas as pl
from jax.experimental.pallas import tpu as pltpu
from jax.sharding import PartitionSpec as P

TOPK = 8
EPS = 1e-06
LOW = -1e30
MESH = pl.DeviceIdType.MESH
F32 = jnp.float32
BF16 = jnp.bfloat16
I32 = jnp.int32
VMEM = pltpu.VMEM
NT = (((1,), (1,)), ((), ()))


def iota(shape, axis):
    return lax.broadcasted_iota(I32, shape, axis)


def coords():
    x = lax.axis_index("query")
    z = lax.axis_index("corpus")
    yc = lax.axis_index("cent")
    return x, z, yc


def at_x(o, n, x):
    return {"query": lax.rem(x + o, n)}


def gather_kernel(X, Z, Y, means, qin, table, qall,
                  ysend, yrecv, qsend, qrecv, rsend, rrecv, lsend, lrecv, psend, precv, lsem):
    x, z, yc = coords()
    y, c = yc // 2, lax.rem(yc, 2)
    rows = table.shape[3]
    half = Z // 2
    up, down = {"corpus": lax.rem(z + 1, Z)}, {"corpus": lax.rem(z + Z - 1, Z)}
    mate = {"cent": y * 2 + 1 - c}

    mine = means.at[pl.ds(x * rows, rows)]
    own_t = pltpu.make_async_copy(mine, table.at[z, y, c], lsem.at[0])
    own_q = pltpu.make_async_copy(qin, qall.at[x], lsem.at[1])
    own_t.start()
    own_q.start()

    bar = pltpu.get_barrier_semaphore()
    peers = [up, down, mate]
    peers += [at_x(o, X, x) for o in range(1, X)]
    peers += [{"cent": lax.rem(y + o, Y) * 2 + c} for o in range(1, Y)]
    for d in peers:
        pl.semaphore_signal(bar, inc=1, device_id=d, device_id_type=MESH)
    pl.semaphore_wait(bar, len(peers))

    def copy(src, dst, s, r, d):
        return pltpu.make_async_remote_copy(
            src_ref=src, dst_ref=dst, send_sem=s, recv_sem=r, device_id=d, device_id_type=MESH)

    ycopies = []
    for o in range(1, Y):
        ycopies.append(copy(mine, table.at[z, y, c], ysend.at[o - 1], yrecv.at[o - 1],
                            {"cent": lax.rem(y + o, Y) * 2 + c}))
        ycopies[-1].start()
    qcopies = []
    for o in range(1, X):
        qcopies.append(copy(qin, qall.at[x], qsend.at[o - 1], qrecv.at[o - 1], at_x(o, X, x)))
        qcopies[-1].start()
    own_t.wait()
    for d in ycopies:
        d.wait_recv()

    hy = Y // 2

    def piece(zo, h):
        return table.at[zo, pl.ds(h * hy, hy), c]

    def to_mate(zo, h):
        copy(piece(zo, h), piece(zo, h), psend.at[0], precv.at[0], mate).start()

    def ring(s, h, right):
        zo = lax.rem(z + Z - s, Z) if right else lax.rem(z + s, Z)
        ss, rr = (rsend, rrecv) if right else (lsend, lrecv)
        return copy(piece(zo, h), piece(zo, h), ss.at[s, h], rr.at[s, h], up if right else down)

    sent = []

    def forward(s, h, right):
        if s + 1 < half or (s + 1 == half and h == (0 if right else 1)):
            d = ring(s, h, right)
            d.start()
            sent.append(d)

    for h in range(2):
        forward(0, h, True)
        forward(0, h, False)
    for h in range(2):
        to_mate(z, h)
    for s in range(1, half + 1):
        for h in range(2):
            for right in (True, False):
                if s == half and h != (0 if right else 1):
                    continue
                zo = lax.rem(z + Z - s, Z) if right else lax.rem(z + s, Z)
                ss, rr = (rsend, rrecv) if right else (lsend, lrecv)
                copy(piece(zo, h), piece(zo, h), ss.at[s - 1, h], rr.at[s - 1, h],
                     up if right else down).wait_recv()
                forward(s, h, right)
                to_mate(zo, h)
    own_q.wait()
    for d in qcopies:
        d.wait()
    for d in ycopies:
        d.wait_send()
    for d in sent:
        d.wait_send()
    whole = copy(table.at[:, :, c], table.at[:, :, 1 - c], psend.at[0], precv.at[0], mate)
    whole.wait_send()
    whole.wait_recv()


def gather_table(X, Z, Y, rows, means, queries):
    n = queries.shape[0]
    dma = pltpu.SemaphoreType.DMA
    half = Z // 2
    return pl.pallas_call(
        functools.partial(gather_kernel, X, Z, Y),
        out_shape=(jax.ShapeDtypeStruct((Z, Y, 2, rows, 128), BF16),
                   jax.ShapeDtypeStruct((X, n, 128), BF16)),
        in_specs=[pl.BlockSpec(memory_space=pl.ANY)] * 2,
        out_specs=(pl.BlockSpec(memory_space=VMEM),) * 2,
        scratch_shapes=[dma((Y - 1,)), dma((Y - 1,)), dma((X - 1,)), dma((X - 1,)),
                        dma((half, 2)), dma((half, 2)), dma((half, 2)), dma((half, 2)),
                        dma((1,)), dma((1,)), dma((2,))],
        compiler_params=pltpu.CompilerParams(
            collective_id=0, has_side_effects=True, vmem_limit_bytes=40 << 20),
        name="gather_table",
    )(means, queries)


def lookup_kernel(X, PP, idx, table, part, wide, got):
    total = table.shape[0]
    step = 512

    def widen(i, carry):
        r = pl.multiple_of(i * step, step)
        wide[pl.ds(r, step), :] = table[pl.ds(r, step), :].astype(F32)
        return carry

    lax.fori_loop(0, total // step, widen, 0)
    wide[pl.ds(total, 8), :] = jnp.zeros((8, 128), F32)

    def pick(i, carry):
        xx, tg = i // 64, lax.rem(i, 64)
        k = lax.rem(tg, 8) * 8 + tg // 8
        at = [idx[xx * PP + j, k] for j in range(PP)]
        rows = [wide[pl.ds(a, 1), :] for a in at]
        base = pl.multiple_of(i * PP, PP)
        for j in range(PP):
            got[pl.ds(base + j, 1), :] = rows[j]
        return carry

    lax.fori_loop(0, X * 64, pick, 0)
    part[...] = got[...].astype(BF16).reshape(part.shape)


def lookup(X, idx, table):
    PP = 64 // X
    total = table.shape[0]
    return pl.pallas_call(
        functools.partial(lookup_kernel, X, PP),
        out_shape=jax.ShapeDtypeStruct((X, 64 * PP, 128), BF16),
        in_specs=[pl.BlockSpec(memory_space=pltpu.SMEM), pl.BlockSpec(memory_space=VMEM)],
        out_specs=pl.BlockSpec(memory_space=VMEM),
        scratch_shapes=[VMEM((total + 8, 128), F32), VMEM((4096, 128), F32)],
        compiler_params=pltpu.CompilerParams(vmem_limit_bytes=40 << 20),
        name="lookup",
    )(idx, table)


def top8(v, base):
    lane = iota(v.shape, 1)
    cum = jnp.zeros((v.shape[0], 1), F32) + base.astype(F32) if not isinstance(base, int) else (
        jnp.full((v.shape[0], 1), float(base), F32))
    first = cum
    lanef = lane.astype(F32)
    out = jnp.zeros(v.shape, F32)
    for _ in range(TOPK):
        m = jnp.max(v, axis=1, keepdims=True)
        eq = v == m
        out = jnp.where(lanef >= cum, m, out)
        cum = cum + jnp.sum(jnp.where(eq, 1.0, 0.0), axis=1, keepdims=True)
        v = jnp.where(eq, -3e38, v)
    return jnp.where((lanef >= first) & (lanef < first + TOPK), out, 0.0)


def score_kernel(X, Z, YC, part, words, amounts, qall, pos, tally, approx, exact, best,
                 rbuf, wbuf, qn, res, dc, df, mp, st, sbuf, c1, c1buf, c2, c2buf,
                 wsem, xsend, xrecv, ssend, srecv, asend, arecv, bsend, brecv):
    x, z, yc = coords()
    PP = 64 // X
    NT_ROWS = 64 * PP
    wcopy = pltpu.make_async_copy(words.at[pl.ds(x * PP, PP)], wbuf, wsem.at[0])
    wcopy.start()

    xpeer = [at_x(o, X, x) for o in range(1, X)]
    cpeer = [{"cent": lax.rem(yc + o, YC)} for o in range(1, YC)]
    zpeer = [{"corpus": lax.rem(z + o, Z)} for o in range(1, Z)]
    bar = pltpu.get_barrier_semaphore()
    for d in zpeer + cpeer + xpeer:
        pl.semaphore_signal(bar, inc=1, device_id=d, device_id_type=MESH)
    pl.semaphore_wait(bar, X + YC + Z - 3)

    def copy(src, dst, s, r, d):
        return pltpu.make_async_remote_copy(
            src_ref=src, dst_ref=dst, send_sem=s, recv_sem=r, device_id=d, device_id_type=MESH)

    xcopies = []
    for o in range(1, X):
        xcopies.append(copy(part.at[lax.rem(x + o, X)], rbuf.at[o - 1],
                            xsend.at[o - 1], xrecv.at[o - 1], xpeer[o - 1]))
        xcopies[-1].start()

    q = qall[...].astype(F32)
    qn[...] = (q * lax.rsqrt(jnp.sum(q * q, axis=1, keepdims=True) + EPS)).astype(BF16)

    wcopy.wait()
    w = jnp.concatenate([wbuf[:, 128 * g:128 * (g + 1)] for g in range(8)], axis=0)
    lo = jnp.bitwise_and(w, 255).astype(F32).astype(BF16)
    hi = jnp.bitwise_and(jnp.right_shift(w, 8), 255).astype(F32).astype(BF16)
    bytes_ = jnp.concatenate([lo, hi], axis=1)
    col = iota((256, 1024), 1)
    d = jnp.bitwise_and(col, 127)
    want = (col // 128) * 16 + d // 8 + jnp.where(jnp.bitwise_and(d, 4) != 0, 128, 0)
    spread = jnp.where(iota((256, 1024), 0) == want, 1.0, 0.0).astype(BF16)
    got = jnp.dot(bytes_, spread, preferred_element_type=F32).astype(I32)
    lane = iota(got.shape, 1)
    low_bit = jnp.left_shift(1, 2 * jnp.bitwise_and(lane, 3))
    b0 = jnp.bitwise_and(got, low_bit) != 0
    b1 = jnp.bitwise_and(got, 2 * low_bit) != 0
    r = jnp.where(b1, jnp.where(b0, amounts[3], amounts[2]), jnp.where(b0, amounts[1], amounts[0]))
    for t in range(8):
        res[pl.ds(t * 8 * PP, 8 * PP), :] = r[:, 128 * t:128 * (t + 1)]

    spos = pos[...].astype(F32).astype(BF16)
    rep = jnp.where(jnp.bitwise_and(iota((16, 128), 1), 15) == iota((16, 128), 0), 1.0, 0.0)
    pos_t = jnp.dot(spos, rep.astype(BF16), preferred_element_type=F32).astype(I32)
    mp[...] = jnp.zeros_like(mp)

    for cp in xcopies:
        cp.wait()

    rows = part[x].astype(F32)
    for o in range(X - 1):
        rows = rows + rbuf[o].astype(F32)
    dc[...] = rows.astype(BF16)
    e = rows + res[...]
    df[...] = (e * lax.rsqrt(jnp.sum(e * e, axis=1, keepdims=True) + EPS)).astype(BF16)

    nq = qn.shape[0]
    blk = 256
    for which, docs in ((0, dc), (1, df)):
        row = pl.multiple_of(which * 64 + x * PP, PP)
        for n in range(nq // blk):
            sim = lax.dot_general(docs[...], qn[n * blk:(n + 1) * blk, :], NT,
                                  preferred_element_type=F32)
            mp[pl.ds(row, PP), n * blk:(n + 1) * blk] = jnp.max(sim.reshape(64, PP, blk), axis=0)
    ones = jnp.where(iota((nq // 32, nq), 1) // 32 == iota((nq // 32, nq), 0), 1.0, 0.0)
    st[...] = lax.dot_general(ones, mp[...], NT, precision=lax.Precision.HIGHEST,
                              preferred_element_type=F32)

    scopies = []
    for o in range(1, X):
        dst = pl.multiple_of(lax.rem(x + o, X) * 16, 16)
        scopies.append(copy(st.at[pl.ds(dst, 16)], sbuf.at[o - 1], ssend.at[o - 1],
                            srecv.at[o - 1], xpeer[o - 1]))
        scopies[-1].start()
    for cp in scopies:
        cp.wait()
    tot = st[pl.ds(pl.multiple_of(x * 16, 16), 16), :]
    for o in range(X - 1):
        tot = tot + sbuf[o]

    lane = iota((16, 128), 1)
    slot = jnp.bitwise_and(lane, 15)
    live = slot < tally[...]
    coarse = jnp.take_along_axis(tot, pos_t, axis=1, mode="promise_in_bounds")
    fine = jnp.take_along_axis(tot, pos_t + 64, axis=1, mode="promise_in_bounds")
    c1[...] = jnp.where(lane // 16 == yc, jnp.where(live, fine, LOW), 0.0)
    acopies = []
    for o in range(1, YC):
        acopies.append(copy(c1, c1buf.at[o - 1], asend.at[o - 1], arecv.at[o - 1], cpeer[o - 1]))
        acopies[-1].start()
    approx[...] = jnp.where(live, coarse, 0.0)[:, :16]
    exact[...] = jnp.where(live, fine, 0.0)[:, :16]
    for cp in acopies:
        cp.wait()
    v = c1[...]
    for o in range(YC - 1):
        v = v + c1buf[o]
    if YC * 16 < 128:
        v = jnp.where(lane < YC * 16, v, -2e38)
    c2[...] = top8(v, z * TOPK)
    bcopies = []
    for o in range(1, Z):
        bcopies.append(copy(c2, c2buf.at[o - 1], bsend.at[o - 1], brecv.at[o - 1], zpeer[o - 1]))
        bcopies[-1].start()
    for cp in bcopies:
        cp.wait()
    v = c2[...]
    for o in range(Z - 1):
        v = v + c2buf[o]
    if Z * TOPK < 128:
        v = jnp.where(lane < Z * TOPK, v, -2e38)
    best[...] = top8(v, 0)[:, :TOPK]


def score(X, Z, YC, part, words, amounts, qall, pos, tally):
    PP = 64 // X
    R = 64 * PP
    nq = qall.shape[0]
    dma = pltpu.SemaphoreType.DMA
    vm = pl.BlockSpec(memory_space=VMEM)
    f = functools.partial(jax.ShapeDtypeStruct, dtype=F32)
    return pl.pallas_call(
        functools.partial(score_kernel, X, Z, YC),
        out_shape=(f((16, 16)), f((16, 16)), f((16, TOPK))),
        in_specs=[vm, pl.BlockSpec(memory_space=pl.ANY), pl.BlockSpec(memory_space=pltpu.SMEM),
                  vm, vm, vm],
        out_specs=(vm, vm, vm),
        scratch_shapes=[
            VMEM((X - 1, R, 128), BF16), VMEM((PP, 1024), I32), VMEM((nq, 128), BF16),
            VMEM((R, 128), F32), VMEM((R, 128), BF16), VMEM((R, 128), BF16),
            VMEM((128, nq), F32), VMEM((nq // 32, 128), F32), VMEM((X - 1, 16, 128), F32),
            VMEM((16, 128), F32), VMEM((YC - 1, 16, 128), F32),
            VMEM((16, 128), F32), VMEM((Z - 1, 16, 128), F32),
            dma((1,)), dma((X - 1,)), dma((X - 1,)), dma((X - 1,)), dma((X - 1,)),
            dma((YC - 1,)), dma((YC - 1,)), dma((Z - 1,)), dma((Z - 1,)),
        ],
        compiler_params=pltpu.CompilerParams(
            collective_id=1, has_side_effects=True, vmem_limit_bytes=40 << 20),
        name="score",
    )(part, words, amounts, qall, pos, tally)


def local(request_term_embeds, cluster_means, cluster_shard_number, cluster_entry_within,
          quantized_error_words, quantized_error_amounts, keeper_document_position,
          active_keeper_tally):
    X, Z, YC = (lax.axis_size(a) for a in ("query", "corpus", "cent"))
    Y = YC // 2
    rows = cluster_means.shape[0] // X
    x = lax.axis_index("query")
    queries = request_term_embeds.reshape(-1, 128)
    table, qall = gather_table(X, Z, Y, rows, cluster_means, queries)
    shard = cluster_shard_number[:, :, 0]
    entry = cluster_entry_within
    idx = jnp.where(entry // rows == x, shard * rows + entry % rows, Z * YC * rows)
    part = lookup(X, idx, table.reshape(-1, 128))
    approx, exact, best = score(
        X, Z, YC, part, quantized_error_words, quantized_error_amounts,
        qall.reshape(-1, 128), keeper_document_position[:, 0, :], active_keeper_tally)
    return approx[:, None, :], exact[:, None, :], best


def solution(mesh):
    return jax.shard_map(
        local,
        mesh=mesh,
        in_specs=(
            P("query", None, None),
            P(("corpus", "cent"), None),
            P(("corpus", "cent"), None, None),
            P(("corpus", "cent"), None),
            P(("corpus", "cent"), None),
            P(),
            P("query", ("corpus", "cent"), None),
            P("query", ("corpus", "cent")),
        ),
        out_specs=(
            P("query", ("corpus", "cent"), None),
            P("query", ("corpus", "cent"), None),
            P("query", None),
        ),
        check_vma=False,
    )
```

time: 669 us -> 115 us (0.17)
  local copies, waits for them, and re-layouts: 188 us -> 7.92 us
  other arithmetic: 164 us -> 0.81 us
  waiting for transfers between devices: 110 us -> 0 us
  Pallas kernels: 0 us -> 105 us
  matrix products: 88.7 us -> 0 us
  blocking collectives: 85.1 us -> 0 us
  starting transfers between devices: 26.4 us -> 0 us
    gather x35 -> x0, local copies, waits for them, and re-layouts: 126 us -> none  [the longest x1 40.2 us: local(): centroid_rows = returned[target_block, slot_rank]]
    all_to_all x2 -> x0, waiting for transfers between devices: 110 us -> none  [the longest x1 95.1 us: local(): lax.all_to_all(looked_up, ('corpus', 'cent'), split_axis=0, concat_axis=0...]
    pallas_call x0 -> x3, Pallas kernels: none -> 105 us  [the longest x1 51 us: gather_table(): pl.pallas_call(functools.partial(gather_kernel, X, Z, Y), out_shape=(jax....]
    top_k x128 -> x0, other arithmetic: 92.8 us -> none  [the longest x127 92 us: keep_best(): lax.top_k(jnp.concatenate([first, second], axis=1), first.shape[1])[0]]
    dot_general x36 -> x0, matrix products: 88.7 us -> none  [the longest x32 60.6 us: maxsim_flat(): jnp.einsum('td,nd->tn', request_embeds, flattened_documents, preferred_el...]
    all_gather x1 -> x0, blocking collectives: 85.1 us -> none  [merged(): pieces = lax.all_gather(value, axis)]
    reduce_sum x50 -> x0, other arithmetic: 52 us -> none  [the longest x17 46.4 us: normalize_rows(): jnp.sum(values * values, axis=-1, keepdims=True) + eps_norm]
    all_to_all x2 -> x0, starting transfers between devices: 26.4 us -> none  [the longest x1 20.6 us: local(): lax.all_to_all(requests, ('corpus', 'cent'), split_axis=0, concat_axis=0,...]
  transfers between devices with their start and end apart: 2 -> 0, of which waited for: 2 -> 0; matrix products, arithmetic and copies ran while one was open for 0% -> 0% of each run, Pallas kernels for 0% -> 0%
where the time goes in v1:
time: 115 us; the launch traced here: 114 us
  Pallas kernels  105 us (91%)
  local copies, waits for them, and re-layouts  7.92 us (7%)
    pallas_call x1, Pallas kernels, gather_table(): pl.pallas_call(functools.partial(gather_kernel, X, Z, Y), out_shape=(jax....  51 us
    pallas_call x1, Pallas kernels, score(): pl.pallas_call(functools.partial(score_kernel, X, Z, YC), out_shape=(f((1...  41.5 us
    pallas_call x1, Pallas kernels, lookup(): pl.pallas_call(functools.partial(lookup_kernel, X, PP), out_shape=jax.Sha...  12 us
    unnamed x20, local copies, waits for them, and re-layouts  7.92 us

profile of v1, /device:TPU:1, one launch (start us, length us, event | category | flops | bytes accessed | tf_op | source)
XLA Modules:
  0.0 114.0 jit_solution(17079159774577161757)
XLA Ops:
  0.6 0.0 copy-start.2
  0.6 0.0 copy-start.3
  0.7 0.9 copy-done.3
  1.6 0.0 copy-start.4
  1.6 0.9 copy-done.4
  2.5 0.0 copy-start.7
  2.5 0.0 copy-start.5
  2.5 0.0 copy-start.6
  2.5 51.0 %gather_table.1 = (bf16[16,4,2,128,128]{4,3,2,1,0:T(8,128)(2,1)S(1)}, bf16[4,512,128]{2,1,0:T(8,128)(2,1)S(1)}) custom-call(bf16[512,128]{1,0:T(8,128)(2,1)S(1)} %copy-done.3, bf16[512,128]{1,0:T(8,128)(2,1)S(1)} %bitcast.15), custom_call_target="tpu_custom_call" | custom-call | tf_op jit(solution)/shard_map/gather_table/pallas_call | solution.py:129
  53.5 0.0 copy-start
  53.6 1.9 %copy-done = bf16[16,4,2,128,128]{4,3,2,1,0:T(8,128)(2,1)} copy-done((bf16[16,4,2,128,128]{4,3,2,1,0:T(8,128)(2,1)}, bf16[16,4,2,128,128]{4,3,2,1,0:T(8,128)(2,1)S(1)}, u32[]{:S(2)}) %copy-start) | copy-done | bytes 4194328
  55.5 0.8 fusion.2.idx
  56.3 0.0 copy-start.1
  56.3 2.2 %copy-done.1 = bf16[16,4,2,128,128]{4,3,2,1,0:T(8,128)(2,1)S(1)} copy-done((bf16[16,4,2,128,128]{4,3,2,1,0:T(8,128)(2,1)S(1)}, bf16[16,4,2,128,128]{4,3,2,1,0:T(8,128)(2,1)}, u32[]{:S(2)}) %copy-start.1) | copy-done | bytes 4194328
  58.5 12.0 %lookup.1.part = bf16[4,1024,128]{2,1,0:T(8,128)(2,1)S(1)} custom-call(s32[64,64]{1,0:T(8,128)S(1)} %fusion.2.idx, bf16[16384,128]{1,0:T(8,128)(2,1)S(1)} %bitcast.13), custom_call_target="tpu_custom_call" | custom-call | tf_op jit(solution)/shard_map/lookup/pallas_call | solution.py:173
  70.5 0.0 copy-done.7
  70.5 0.1 copy.12.tally
  70.6 0.0 copy-done.2
  70.6 0.0 copy-done.5
  70.6 0.0 copy-done.6
  70.6 41.5 %score.1 = (f32[16,16]{1,0:T(8,128)S(1)}, f32[16,16]{1,0:T(8,128)S(1)}, f32[16,8]{1,0:T(8,128)S(1)}) custom-call(bf16[4,1024,128]{2,1,0:T(8,128)(2,1)S(1)} %lookup.1.part, s32[64,1024]{1,0:T(8,128)S(1)} %copy-done.2, f32[4]{0:T(128)S(1)} %copy-done.6, bf16[2048,128]{1,0:T(8,128)(2,1)S(1)} %bitcast.14, s32[16,16]{1,0:T(8,128)S(1)} %bitcast.16, ...), custom_call_target="tpu_custom_call" | custom-call | tf_op jit(solution)/shard_map/score/pallas_call | solution.py:328
  112.1 0.7 copy.15
  112.8 0.6 copy.18
  113.4 0.6 copy.19
Async XLA Ops:
  0.6 69.9 %copy-start.2 = (s32[64,1024]{1,0:T(8,128)S(1)}, s32[64,1024]{1,0:T(8,128)}, u32[]{:S(2)}) copy-start(s32[64,1024]{1,0:T(8,128)} %words.1) | copy-start | bytes 786436
  0.6 0.9 copy-start.3
  1.6 0.9 copy-start.4
  2.5 68.0 %copy-start.7 = (s32[16,1]{0,1:T(1,128)S(1)}, s32[16,1]{0,1:T(1,128)}, u32[]{:S(2)}) copy-start(s32[16,1]{0,1:T(1,128)} %param.15) | copy-start | bytes 196
  2.5 68.1 %copy-start.5 = (s32[16,1,16]{2,1,0:T(1,128)S(1)}, s32[16,1,16]{2,1,0:T(1,128)}, u32[]{:S(2)}) copy-start(s32[16,1,16]{2,1,0:T(1,128)} %param.14) | copy-start | bytes 3076
  2.5 68.1 %copy-start.6 = (f32[4]{0:T(128)S(1)}, f32[4]{0:T(128)}, u32[]{:S(2)}) copy-start(f32[4]{0:T(128)} %amounts.1) | copy-start | bytes 52
  53.5 1.9 %copy-start = (bf16[16,4,2,128,128]{4,3,2,1,0:T(8,128)(2,1)}, bf16[16,4,2,128,128]{4,3,2,1,0:T(8,128)(2,1)S(1)}, u32[]{:S(2)}) copy-start(bf16[16,4,2,128,128]{4,3,2,1,0:T(8,128)(2,1)S(1)} %get-tuple-element.8) | copy-start | bytes 12582916
  56.3 2.2 %copy-start.1 = (bf16[16,4,2,128,128]{4,3,2,1,0:T(8,128)(2,1)S(1)}, bf16[16,4,2,128,128]{4,3,2,1,0:T(8,128)(2,1)}, u32[]{:S(2)}) copy-start(bf16[16,4,2,128,128]{4,3,2,1,0:T(8,128)(2,1)} %copy-done) | copy-start | bytes 12582916

commit v2 on v0

v2 whole, which is shorter than its diff:
```python
import collections
import functools

import jax
import jax.numpy as jnp
from jax import lax
from jax.experimental import pallas as pl
from jax.experimental.pallas import tpu as pltpu
from jax.sharding import PartitionSpec as P

TOPK = 8
EPS = 1e-06
LOW = -1e30
MESH = pl.DeviceIdType.MESH
F32 = jnp.float32
BF16 = jnp.bfloat16
I32 = jnp.int32
VMEM = pltpu.VMEM
NT = (((1,), (1,)), ((), ()))
CHUNKS = 4


def iota(shape, axis):
    return lax.broadcasted_iota(I32, shape, axis)


def remote(src, dst, s, r, d):
    return pltpu.make_async_remote_copy(
        src_ref=src, dst_ref=dst, send_sem=s, recv_sem=r, device_id=d, device_id_type=MESH)


def top8(v, base):
    lane = iota(v.shape, 1).astype(F32)
    first = jnp.zeros((v.shape[0], 1), F32) + jnp.asarray(base).astype(F32)
    cum = first
    out = jnp.zeros(v.shape, F32)
    for _ in range(TOPK):
        m = jnp.max(v, axis=1, keepdims=True)
        eq = v == m
        out = jnp.where(lane >= cum, m, out)
        cum = cum + jnp.sum(jnp.where(eq, 1.0, 0.0), axis=1, keepdims=True)
        v = jnp.where(eq, -3e38, v)
    return jnp.where((lane >= first) & (lane < first + TOPK), out, 0.0)


def kernel(X, Z, Y, means, qin, shard, entry, words, amounts, pos, tally, out,
           table, wide, qall, qn, shard_v, entry_v, idx_v, idx, wbuf, spread, res, got, own,
           part, rbuf, dc, df, mp, st, sbuf, c1, c1buf, c2, c2buf,
           lsem, rsend, rrecv, lsend, lrecv, ysend, yrecv, qsend, qrecv, psend, precv,
           xsend, xrecv, ssend, srecv, asend, arecv, bsend, brecv):
    x = lax.axis_index("query")
    z = lax.axis_index("corpus")
    yc = lax.axis_index("cent")
    YC = 2 * Y
    y, c = yc // 2, lax.rem(yc, 2)
    PP = 64 // X
    rows = table.shape[3]
    hr = rows // 2
    half = Z // 2
    total = Z * YC * rows
    R = 64 * PP
    CR = R // CHUNKS

    mine = means.at[pl.ds(x * rows, rows)]
    locals_ = [
        pltpu.make_async_copy(mine, table.at[z, y, c], lsem.at[0]),
        pltpu.make_async_copy(qin, qall.at[x], lsem.at[1]),
        pltpu.make_async_copy(shard, shard_v, lsem.at[2]),
        pltpu.make_async_copy(entry, entry_v, lsem.at[3]),
        pltpu.make_async_copy(words.at[pl.ds(x * PP, PP)], wbuf, lsem.at[4]),
    ]
    for d in locals_:
        d.start()

    up, down = {"corpus": lax.rem(z + 1, Z)}, {"corpus": lax.rem(z + Z - 1, Z)}
    mate = {"cent": y * 2 + 1 - c}
    ypeer = [{"cent": lax.rem(y + o, Y) * 2 + c} for o in range(1, Y)]
    xpeer = [{"query": lax.rem(x + o, X)} for o in range(1, X)]
    cpeer = [{"cent": lax.rem(yc + o, YC)} for o in range(1, YC)]
    zpeer = [{"corpus": lax.rem(z + o, Z)} for o in range(1, Z)]
    bar = pltpu.get_barrier_semaphore()
    near = [up, down, mate] + ypeer + xpeer
    for d in near:
        pl.semaphore_signal(bar, inc=1, device_id=d, device_id_type=MESH)
    pl.semaphore_wait(bar, len(near))

    def origin(s, right):
        return lax.rem(z + Z - s, Z) if right else lax.rem(z + s, Z)

    def ref(zo, yo, h):
        return table.at[zo, yo, c, pl.ds(h * hr, hr)]

    def last(h, right):
        return half if (h == 0) == right else half - 1

    def ring(h, s, right):
        r = ref(origin(s, right), y, h)
        return remote(r, r, (rsend if right else lsend).at[h, s], (rrecv if right else lrecv).at[h, s],
                      up if right else down)

    def slot(s, right):
        return s if right else half + s

    def ycopy(h, s, right, o, back):
        yo = lax.rem(y + Y - o, Y) if back else y
        r = ref(origin(s, right), yo, h)
        return remote(r, r, ysend.at[o - 1], yrecv.at[h, slot(s, right), o - 1], ypeer[o - 1])

    def widen(zo, yo, h, cc, n):
        base = pl.multiple_of(((zo * Y + yo) * 2 + cc) * rows + h * hr, hr)
        wide[pl.ds(base, n), :] = table[zo, yo, cc, pl.ds(h * hr, n), :].astype(F32)

    def to_mate(zo, yo, h):
        r = ref(zo, yo, h)
        remote(r, r, psend.at[0], precv.at[0], mate).start()

    sent = []
    pending = collections.deque()

    def forward(h, s, right):
        if s < last(h, right):
            d = ring(h, s, right)
            d.start()
            sent.append(d)

    def spread_out(h, s, right):
        for o in range(1, Y):
            ycopy(h, s, right, o, False).start()
        pending.append((h, s, right))
        to_mate(origin(s, right), y, h)

    def collect(upto):
        while pending and pending[0][1] <= upto:
            h, s, right = pending.popleft()
            for o in range(1, Y):
                ycopy(h, s, right, o, True).wait_recv()
                yo = lax.rem(y + Y - o, Y)
                to_mate(origin(s, right), yo, h)
                widen(origin(s, right), yo, h, c, hr)

    def make_index():
        locals_[2].wait()
        locals_[3].wait()
        e = entry_v[...]
        idx_v[...] = jnp.where(e // rows == x, shard_v[...] * rows + lax.rem(e, rows), total)
        for o in range(X):
            src = idx_v.at[pl.ds(pl.multiple_of(lax.rem(x + o, X) * PP, PP), PP)]
            pltpu.make_async_copy(src, idx.at[pl.ds(o * PP, PP)], lsem.at[5 + o]).start()
        wide[pl.ds(total, 8), :] = jnp.zeros((8, 128), F32)

    def make_spread():
        col = iota((256, 1024), 1)
        d = jnp.bitwise_and(col, 127)
        want = (col // 128) * 16 + d // 8 + jnp.where(jnp.bitwise_and(d, 4) != 0, 128, 0)
        spread[...] = jnp.where(iota((256, 1024), 0) == want, 1.0, 0.0).astype(BF16)

    def decode():
        locals_[4].wait()
        w = jnp.concatenate([wbuf[:, 128 * g:128 * (g + 1)] for g in range(8)], axis=0)
        lo = jnp.bitwise_and(w, 255).astype(F32).astype(BF16)
        hi = jnp.bitwise_and(jnp.right_shift(w, 8), 255).astype(F32).astype(BF16)
        code = jnp.dot(jnp.concatenate([lo, hi], axis=1), spread[...],
                       preferred_element_type=F32).astype(I32)
        bit = jnp.left_shift(1, 2 * jnp.bitwise_and(iota(code.shape, 1), 3))
        b0 = jnp.bitwise_and(code, bit) != 0
        b1 = jnp.bitwise_and(code, 2 * bit) != 0
        r = jnp.where(b1, jnp.where(b0, amounts[3], amounts[2]), jnp.where(b0, amounts[1], amounts[0]))
        for t in range(8):
            res[pl.ds(t * 8 * PP, 8 * PP), :] = r[:, 128 * t:128 * (t + 1)]

    def normalize(k):
        q = qall[k].astype(F32)
        n = q.shape[0]
        qn[pl.ds(pl.multiple_of(k * n, n), n), :] = (
            q * lax.rsqrt(jnp.sum(q * q, axis=1, keepdims=True) + EPS)).astype(BF16)

    def normalize_own():
        locals_[1].wait()
        normalize(x)

    def normalize_peer(o):
        remote(qin, qall.at[x], qsend.at[o - 1], qrecv.at[o - 1], xpeer[o - 1]).wait()
        normalize(lax.rem(x + X - o, X))

    work = collections.deque([make_index, make_spread, decode, normalize_own] +
                             [functools.partial(normalize_peer, o) for o in range(1, X)])

    locals_[0].wait()
    for h in range(2):
        forward(h, 0, True)
        forward(h, 0, False)
    for o in range(1, X):
        remote(qin, qall.at[x], qsend.at[o - 1], qrecv.at[o - 1], xpeer[o - 1]).start()
    for h in range(2):
        spread_out(h, 0, True)
    widen(z, y, 0, c, rows)
    work.popleft()()
    for s in range(1, half + 1):
        for h in range(2):
            for right in (True, False):
                if s <= last(h, right):
                    r = ref(origin(s, right), y, h)
                    remote(r, r, (rsend if right else lsend).at[h, s - 1],
                           (rrecv if right else lrecv).at[h, s - 1], up if right else down).wait_recv()
                    forward(h, s, right)
                    spread_out(h, s, right)
                    widen(origin(s, right), y, h, c, hr)
        if work:
            work.popleft()()
        collect(s - 2)
    while work:
        work.popleft()()
    collect(half)
    whole = remote(table.at[:, :, c], table.at[:, :, 1 - c], psend.at[0], precv.at[0], mate)
    whole.wait_recv()

    def widen_mate(i, carry):
        for yo in range(Y):
            widen(i, yo, 0, 1 - c, rows)
        return carry

    lax.fori_loop(0, Z, widen_mate, 0)
    for o in range(X):
        pltpu.make_async_copy(idx_v.at[pl.ds(0, PP)], idx.at[pl.ds(o * PP, PP)], lsem.at[5 + o]).wait()

    tc = 8 // CHUNKS

    def xcopy(o, ch):
        piece = pl.ds(ch * CR, CR)
        return remote(part.at[o - 1, piece], rbuf.at[o - 1, piece], xsend.at[o - 1, ch],
                      xrecv.at[o - 1, ch], xpeer[o - 1])

    order = [o for o in (2, 1, 3) if o < X] + [o for o in range(4, X)]
    for ch in range(CHUNKS):
        for o in order + [0]:
            def pick(g, carry, o=o, ch=ch):
                for t in range(tc):
                    k = 8 * g + ch * tc + t
                    picked = [wide[pl.ds(idx[o * PP + j, k], 1), :] for j in range(PP)]
                    base = pl.multiple_of(g * PP + t * 8 * PP, PP)
                    for j in range(PP):
                        if o:
                            got[pl.ds(base + j, 1), :] = picked[j]
                        else:
                            own[pl.ds(base + ch * CR + j, 1), :] = picked[j]
                return carry

            lax.fori_loop(0, 8, pick, 0)
            if o:
                part[o - 1, ch * CR:(ch + 1) * CR, :] = got[...].astype(BF16)
                xcopy(o, ch).start()

    mp[...] = jnp.zeros_like(mp)
    nq = qn.shape[0]
    blk = 256
    for ch in range(CHUNKS):
        a, b = ch * CR, (ch + 1) * CR
        v = own[a:b, :]
        for o in order:
            xcopy(o, ch).wait()
            v = v + rbuf[o - 1, a:b, :].astype(F32)
        dc[...] = v.astype(BF16)
        e = v + res[a:b, :]
        df[...] = (e * lax.rsqrt(jnp.sum(e * e, axis=1, keepdims=True) + EPS)).astype(BF16)
        for which, docs in ((0, dc), (1, df)):
            row = pl.multiple_of(which * 64 + x * PP, PP)
            for n in range(nq // blk):
                sim = lax.dot_general(docs[...], qn[n * blk:(n + 1) * blk, :], NT,
                                      preferred_element_type=F32)
                m = jnp.max(sim.reshape(CR // PP, PP, blk), axis=0)
                if ch:
                    m = jnp.maximum(m, mp[pl.ds(row, PP), n * blk:(n + 1) * blk])
                mp[pl.ds(row, PP), n * blk:(n + 1) * blk] = m
    ones = jnp.where(iota((nq // 32, nq), 1) // 32 == iota((nq // 32, nq), 0), 1.0, 0.0)
    st[...] = lax.dot_general(ones, mp[...], NT, precision=lax.Precision.HIGHEST,
                              preferred_element_type=F32)

    scopies = []
    for o in range(1, X):
        dst = pl.multiple_of(lax.rem(x + o, X) * 16, 16)
        scopies.append(remote(st.at[pl.ds(dst, 16)], sbuf.at[o - 1], ssend.at[o - 1],
                              srecv.at[o - 1], xpeer[o - 1]))
        scopies[-1].start()

    lane = iota((16, 128), 1)
    rep = jnp.where(jnp.bitwise_and(lane, 15) == iota((16, 128), 0), 1.0, 0.0).astype(BF16)
    pos_t = jnp.dot(pos[...].astype(F32).astype(BF16), rep, preferred_element_type=F32).astype(I32)
    count = jnp.sum(jnp.where(iota((16, 16), 0) == iota((16, 16), 1), tally[...], 0),
                    axis=1, keepdims=True)
    live = jnp.bitwise_and(lane, 15) < count
    for cp in scopies:
        cp.wait()
    tot = st[pl.ds(pl.multiple_of(x * 16, 16), 16), :]
    for o in range(X - 1):
        tot = tot + sbuf[o]
    fine = jnp.take_along_axis(tot, pos_t + 64, axis=1, mode="promise_in_bounds")
    c1[...] = jnp.where(lane // 16 == yc, jnp.where(live, fine, LOW), 0.0)
    acopies = []
    for o in range(1, YC):
        acopies.append(remote(c1, c1buf.at[o - 1], asend.at[o - 1], arecv.at[o - 1], cpeer[o - 1]))
        acopies[-1].start()
    coarse = jnp.take_along_axis(tot, pos_t, axis=1, mode="promise_in_bounds")
    scores = jnp.where(live, jnp.where(lane < 16, coarse, fine), 0.0)
    for cp in acopies:
        cp.wait()
    v = c1[...]
    for o in range(YC - 1):
        v = v + c1buf[o]
    c2[...] = top8(v, z * TOPK)
    bcopies = []
    for o in range(1, Z):
        bcopies.append(remote(c2, c2buf.at[o - 1], bsend.at[o - 1], brecv.at[o - 1], zpeer[o - 1]))
        bcopies[-1].start()
    for d in sent:
        d.wait_send()
    for o in range(1, Y):
        r = table.at[:, y, c]
        remote(r, r, ysend.at[o - 1], yrecv.at[0, 0, o - 1], ypeer[o - 1]).wait_send()
    whole.wait_send()
    for cp in bcopies:
        cp.wait()
    v = c2[...]
    for o in range(Z - 1):
        v = v + c2buf[o]
    out[...] = jnp.where(lane < 32, scores, top8(v, 32))


def fused(X, Z, YC, means, queries, shard, entry, words, amounts, pos, tally):
    PP = 64 // X
    R = 64 * PP
    CR = R // CHUNKS
    Y = YC // 2
    rows = means.shape[0] // X
    half = Z // 2
    n = queries.shape[0]
    nq = X * n
    dma = pltpu.SemaphoreType.DMA
    vm = pl.BlockSpec(memory_space=VMEM)
    hbm = pl.BlockSpec(memory_space=pltpu.HBM)
    return pl.pallas_call(
        functools.partial(kernel, X, Z, Y),
        out_shape=jax.ShapeDtypeStruct((16, 128), F32),
        in_specs=[hbm, hbm, hbm, hbm, hbm, pl.BlockSpec(memory_space=pltpu.SMEM), vm, vm],
        out_specs=vm,
        scratch_shapes=[
            VMEM((Z, Y, 2, rows, 128), BF16), VMEM((Z * YC * rows + 8, 128), F32),
            VMEM((X, n, 128), BF16), VMEM((nq, 128), BF16),
            VMEM((64, 64), I32), VMEM((64, 64), I32), VMEM((64, 64), I32),
            pltpu.SMEM((64, 64), I32), VMEM((PP, 1024), I32), VMEM((256, 1024), BF16),
            VMEM((R, 128), F32), VMEM((CR, 128), F32), VMEM((R, 128), F32),
            VMEM((X - 1, R, 128), BF16), VMEM((X - 1, R, 128), BF16),
            VMEM((CR, 128), BF16), VMEM((CR, 128), BF16),
            VMEM((128, nq), F32), VMEM((nq // 32, 128), F32), VMEM((X - 1, 16, 128), F32),
            VMEM((16, 128), F32), VMEM((YC - 1, 16, 128), F32),
            VMEM((16, 128), F32), VMEM((Z - 1, 16, 128), F32),
            dma((5 + X,)),
            dma((2, half)), dma((2, half)), dma((2, half)), dma((2, half)),
            dma((Y - 1,)), dma((2, 2 * half + 1, Y - 1)),
            dma((X - 1,)), dma((X - 1,)), dma((1,)), dma((1,)),
            dma((X - 1, CHUNKS)), dma((X - 1, CHUNKS)), dma((X - 1,)), dma((X - 1,)),
            dma((YC - 1,)), dma((YC - 1,)), dma((Z - 1,)), dma((Z - 1,)),
        ],
        compiler_params=pltpu.CompilerParams(
            collective_id=0, has_side_effects=True, vmem_limit_bytes=60 << 20),
        name="plaid",
    )(means, queries, shard, entry, words, amounts, pos, tally)


def local(request_term_embeds, cluster_means, cluster_shard_number, cluster_entry_within,
          quantized_error_words, quantized_error_amounts, keeper_document_position,
          active_keeper_tally):
    X, Z, YC = (lax.axis_size(a) for a in ("query", "corpus", "cent"))
    out = fused(X, Z, YC, cluster_means, request_term_embeds.reshape(-1, 128),
                cluster_shard_number[:, :, 0], cluster_entry_within, quantized_error_words,
                quantized_error_amounts, keeper_document_position[:, 0, :],
                active_keeper_tally.reshape(1, 16))
    return out[:, None, 0:16], out[:, None, 16:32], out[:, 32:32 + TOPK]


def solution(mesh):
    return jax.shard_map(
        local,
        mesh=mesh,
        in_specs=(
            P("query", None, None),
            P(("corpus", "cent"), None),
            P(("corpus", "cent"), None, None),
            P(("corpus", "cent"), None),
            P(("corpus", "cent"), None),
            P(),
            P("query", ("corpus", "cent"), None),
            P("query", ("corpus", "cent")),
        ),
        out_specs=(
            P("query", ("corpus", "cent"), None),
            P("query", ("corpus", "cent"), None),
            P("query", None),
        ),
        check_vma=False,
    )
```

time: 669 us -> 83.2 us (0.12)
  local copies, waits for them, and re-layouts: 188 us -> 2.14 us
  other arithmetic: 164 us -> 0 us
  waiting for transfers between devices: 110 us -> 0 us
  matrix products: 88.7 us -> 0 us
  blocking collectives: 85.1 us -> 0 us
  Pallas kernels: 0 us -> 80.2 us
  starting transfers between devices: 26.4 us -> 0 us
    gather x35 -> x0, local copies, waits for them, and re-layouts: 126 us -> none  [the longest x1 40.2 us: local(): centroid_rows = returned[target_block, slot_rank]]
    all_to_all x2 -> x0, waiting for transfers between devices: 110 us -> none  [the longest x1 95.1 us: local(): lax.all_to_all(looked_up, ('corpus', 'cent'), split_axis=0, concat_axis=0...]
    top_k x128 -> x0, other arithmetic: 92.8 us -> none  [the longest x127 92 us: keep_best(): lax.top_k(jnp.concatenate([first, second], axis=1), first.shape[1])[0]]
    dot_general x36 -> x0, matrix products: 88.7 us -> none  [the longest x32 60.6 us: maxsim_flat(): jnp.einsum('td,nd->tn', request_embeds, flattened_documents, preferred_el...]
    all_gather x1 -> x0, blocking collectives: 85.1 us -> none  [merged(): pieces = lax.all_gather(value, axis)]
    pallas_call x0 -> x1, Pallas kernels: none -> 80.2 us  [fused(): pl.pallas_call(functools.partial(kernel, X, Z, Y), out_shape=jax.ShapeDty...]
    reduce_sum x50 -> x0, other arithmetic: 52 us -> none  [the longest x17 46.4 us: normalize_rows(): jnp.sum(values * values, axis=-1, keepdims=True) + eps_norm]
    all_to_all x2 -> x0, starting transfers between devices: 26.4 us -> none  [the longest x1 20.6 us: local(): lax.all_to_all(requests, ('corpus', 'cent'), split_axis=0, concat_axis=0,...]
  transfers between devices with their start and end apart: 2 -> 0, of which waited for: 2 -> 0; matrix products, arithmetic and copies ran while one was open for 0% -> 0% of each run, Pallas kernels for 0% -> 0%
where the time goes in v2:
time: 83.2 us; the launch traced here: 82.9 us
  Pallas kernels  80.2 us (96%)
  local copies, waits for them, and re-layouts  2.14 us (3%)
    pallas_call x1, Pallas kernels, fused(): pl.pallas_call(functools.partial(kernel, X, Z, Y), out_shape=jax.ShapeDty...  80.2 us

profile of v2, /device:TPU:1, one launch (start us, length us, event | category | flops | bytes accessed | tf_op | source)
XLA Modules:
  0.0 82.9 jit_solution(13412357905760588650)
XLA Ops:
  0.6 80.2 %plaid.1 = f32[16,128]{1,0:T(8,128)} custom-call(bf16[512,128]{1,0:T(8,128)(2,1)} %means.1, bf16[512,128]{1,0:T(8,128)(2,1)} %bitcast.10, s32[64,64]{1,0:T(8,128)} %bitcast.11, s32[64,64]{1,0:T(8,128)} %entry.1, s32[64,1024]{1,0:T(8,128)} %words.1, f32[4]{0:T(128)} %amounts.1, s32[16,16]{1,0:T(8,128)} %bitcast.12, s32[1,16]{1,0:T(1,128)} %bitcast.15), custom_call_target="tpu_custom_call" | custom-call | tf_op jit(solution)/shard_map/plaid/pallas_call | solution.py:340
  80.8 0.8 slice.11
  81.6 0.0 copy-start
  81.6 0.7 copy.13
  82.2 0.0 copy-done
  82.3 0.7 fusion
Async XLA Ops:
  81.6 0.7 copy-start

commit v3 on v2

--- a/solution.py
+++ b/solution.py
@@ -29,24 +29,25 @@
         src_ref=src, dst_ref=dst, send_sem=s, recv_sem=r, device_id=d, device_id_type=MESH)
 
 
-def top8(v, base):
-    lane = iota(v.shape, 1).astype(F32)
-    first = jnp.zeros((v.shape[0], 1), F32) + jnp.asarray(base).astype(F32)
+def top8(vs, base):
+    lane = iota(vs[0].shape, 1).astype(F32)
+    first = jnp.zeros((vs[0].shape[0], 1), F32) + base
     cum = first
-    out = jnp.zeros(v.shape, F32)
+    out = jnp.zeros(vs[0].shape, F32)
     for _ in range(TOPK):
-        m = jnp.max(v, axis=1, keepdims=True)
-        eq = v == m
+        m = jnp.max(functools.reduce(jnp.maximum, vs), axis=1, keepdims=True)
         out = jnp.where(lane >= cum, m, out)
-        cum = cum + jnp.sum(jnp.where(eq, 1.0, 0.0), axis=1, keepdims=True)
-        v = jnp.where(eq, -3e38, v)
+        equal = [v == m for v in vs]
+        seen = functools.reduce(jnp.add, [jnp.where(e, 1.0, 0.0) for e in equal])
+        cum = cum + jnp.sum(seen, axis=1, keepdims=True)
+        vs = [jnp.where(e, -3e38, v) for e, v in zip(equal, vs)]
     return jnp.where((lane >= first) & (lane < first + TOPK), out, 0.0)
 
 
 def kernel(X, Z, Y, means, qin, shard, entry, words, amounts, pos, tally, out,
            table, wide, qall, qn, shard_v, entry_v, idx_v, idx, wbuf, spread, res, got, own,
-           part, rbuf, dc, df, mp, st, sbuf, c1, c1buf, c2, c2buf,
-           lsem, rsend, rrecv, lsend, lrecv, ysend, yrecv, qsend, qrecv, psend, precv,
+           part, rbuf, dc, df, mp, st, sbuf, pos_all, tal_all, keep, c1, c1buf, c2, c2buf,
+           lsem, rsend, rrecv, lsend, lrecv, ysend, yrecv, qsend, qrecv, psend, precv, tsend, trecv,
            xsend, xrecv, ssend, srecv, asend, arecv, bsend, brecv):
     x = lax.axis_index("query")
     z = lax.axis_index("corpus")
@@ -72,14 +73,13 @@
     for d in locals_:
         d.start()
 
-    up, down = {"corpus": lax.rem(z + 1, Z)}, {"corpus": lax.rem(z + Z - 1, Z)}
+    zdev = {(k, r): {"corpus": lax.rem(z + (k if r else Z - k), Z)} for k in (1, 2) for r in (True, False)}
     mate = {"cent": y * 2 + 1 - c}
     ypeer = [{"cent": lax.rem(y + o, Y) * 2 + c} for o in range(1, Y)]
     xpeer = [{"query": lax.rem(x + o, X)} for o in range(1, X)]
-    cpeer = [{"cent": lax.rem(yc + o, YC)} for o in range(1, YC)]
     zpeer = [{"corpus": lax.rem(z + o, Z)} for o in range(1, Z)]
     bar = pltpu.get_barrier_semaphore()
-    near = [up, down, mate] + ypeer + xpeer
+    near = list(zdev.values()) + [mate] + ypeer + xpeer
     for d in near:
         pl.semaphore_signal(bar, inc=1, device_id=d, device_id_type=MESH)
     pl.semaphore_wait(bar, len(near))
@@ -93,18 +93,17 @@
     def last(h, right):
         return half if (h == 0) == right else half - 1
 
-    def ring(h, s, right):
+    def ring(h, s, right, hop):
         r = ref(origin(s, right), y, h)
-        return remote(r, r, (rsend if right else lsend).at[h, s], (rrecv if right else lrecv).at[h, s],
-                      up if right else down)
+        return remote(r, r, (rsend if right else lsend).at[h, s + hop - 1],
+                      (rrecv if right else lrecv).at[h, s + hop - 1], zdev[hop, right])
 
     def slot(s, right):
         return s if right else half + s
 
-    def ycopy(h, s, right, o, back):
-        yo = lax.rem(y + Y - o, Y) if back else y
+    def ycopy(h, s, right, yo, to, tag):
         r = ref(origin(s, right), yo, h)
-        return remote(r, r, ysend.at[o - 1], yrecv.at[h, slot(s, right), o - 1], ypeer[o - 1])
+        return remote(r, r, ysend.at[tag - 1], yrecv.at[h, slot(s, right), tag - 1], ypeer[to - 1])
 
     def widen(zo, yo, h, cc, n):
         base = pl.multiple_of(((zo * Y + yo) * 2 + cc) * rows + h * hr, hr)
@@ -115,28 +114,39 @@
         remote(r, r, psend.at[0], precv.at[0], mate).start()
 
     sent = []
-    pending = collections.deque()
-
-    def forward(h, s, right):
-        if s < last(h, right):
-            d = ring(h, s, right)
+    pending, relayed = collections.deque(), collections.deque()
+
+    def forward(h, s, right, hop):
+        if s + hop <= last(h, right):
+            d = ring(h, s, right, hop)
             d.start()
             sent.append(d)
 
-    def spread_out(h, s, right):
-        for o in range(1, Y):
-            ycopy(h, s, right, o, False).start()
+    def along_y(h, s, right):
+        for o in (1, Y - 1):
+            ycopy(h, s, right, y, o, o).start()
         pending.append((h, s, right))
-        to_mate(origin(s, right), y, h)
 
     def collect(upto):
         while pending and pending[0][1] <= upto:
             h, s, right = pending.popleft()
-            for o in range(1, Y):
-                ycopy(h, s, right, o, True).wait_recv()
-                yo = lax.rem(y + Y - o, Y)
-                to_mate(origin(s, right), yo, h)
-                widen(origin(s, right), yo, h, c, hr)
+            for o in (1, Y - 1):
+                ycopy(h, s, right, lax.rem(y + Y - o, Y), o, o).wait_recv()
+                if (h == 0) == (o == 1):
+                    ycopy(h, s, right, lax.rem(y + Y - o, Y), o, 2).start()
+            for o in (1, Y - 1):
+                to_mate(origin(s, right), lax.rem(y + Y - o, Y), h)
+            for o in (1, Y - 1):
+                widen(origin(s, right), lax.rem(y + Y - o, Y), h, c, hr)
+            relayed.append((h, s, right))
+
+    def collect_relayed(upto):
+        while relayed and relayed[0][1] <= upto:
+            h, s, right = relayed.popleft()
+            yo = lax.rem(y + 2, Y)
+            ycopy(h, s, right, yo, 1, 2).wait_recv()
+            to_mate(origin(s, right), yo, h)
+            widen(origin(s, right), yo, h, c, hr)
 
     def make_index():
         locals_[2].wait()
@@ -182,35 +192,75 @@
         remote(qin, qall.at[x], qsend.at[o - 1], qrecv.at[o - 1], xpeer[o - 1]).wait()
         normalize(lax.rem(x + X - o, X))
 
-    work = collections.deque([make_index, make_spread, decode, normalize_own] +
+    lane = iota((16, 128), 1)
+    fine0 = 64 * c + PP * x
+    coarse0 = 64 * (1 - c) + PP * x
+
+    def keep_rows(k):
+        p = pos_all[k]
+        count = jnp.sum(jnp.where(iota((16, 16), 0) == iota((16, 16), 1), tal_all[k], 0),
+                        axis=1, keepdims=True)
+        p = jnp.where(iota((16, 16), 1) < count, p, -1000)
+        kept = jnp.zeros((16, 128), I32)
+        for j in range(16):
+            kept = jnp.where(p[:, j:j + 1] - PP * x == lane - fine0, 1, kept)
+        kept = jnp.where((lane >= fine0) & (lane < fine0 + PP), kept, 2)
+        keep[pl.ds(pl.multiple_of(k * 16, 16), 16), :] = kept
+
+    def keep_peer(o):
+        remote(pos, pos_all.at[x], tsend.at[0, o - 1], trecv.at[0, o - 1], xpeer[o - 1]).wait()
+        remote(tally, tal_all.at[x], tsend.at[1, o - 1], trecv.at[1, o - 1], xpeer[o - 1]).wait()
+        keep_rows(lax.rem(x + X - o, X))
+
+    def keep_own():
+        pos_all[x] = pos[...]
+        tal_all[x] = tally[...]
+        keep_rows(x)
+
+    def keep_all():
+        keep_own()
+        for o in range(1, X):
+            keep_peer(o)
+
+    work = collections.deque([make_index, make_spread, keep_all, decode, normalize_own] +
                              [functools.partial(normalize_peer, o) for o in range(1, X)])
 
     locals_[0].wait()
+    for hop in (1, 2):
+        for h in range(2):
+            forward(h, 0, True, hop)
+            forward(h, 0, False, hop)
     for h in range(2):
-        forward(h, 0, True)
-        forward(h, 0, False)
+        along_y(h, 0, True)
     for o in range(1, X):
+        remote(pos, pos_all.at[x], tsend.at[0, o - 1], trecv.at[0, o - 1], xpeer[o - 1]).start()
+        remote(tally, tal_all.at[x], tsend.at[1, o - 1], trecv.at[1, o - 1], xpeer[o - 1]).start()
         remote(qin, qall.at[x], qsend.at[o - 1], qrecv.at[o - 1], xpeer[o - 1]).start()
     for h in range(2):
-        spread_out(h, 0, True)
+        to_mate(z, y, h)
     widen(z, y, 0, c, rows)
     work.popleft()()
     for s in range(1, half + 1):
-        for h in range(2):
-            for right in (True, False):
-                if s <= last(h, right):
-                    r = ref(origin(s, right), y, h)
-                    remote(r, r, (rsend if right else lsend).at[h, s - 1],
-                           (rrecv if right else lrecv).at[h, s - 1], up if right else down).wait_recv()
-                    forward(h, s, right)
-                    spread_out(h, s, right)
-                    widen(origin(s, right), y, h, c, hr)
+        here = [(h, right) for h in range(2) for right in (True, False) if s <= last(h, right)]
+        for h, right in here:
+            r = ref(origin(s, right), y, h)
+            remote(r, r, (rsend if right else lsend).at[h, s - 1],
+                   (rrecv if right else lrecv).at[h, s - 1], zdev[1, right]).wait_recv()
+            forward(h, s, right, 2)
+        for h, right in here:
+            along_y(h, s, right)
+        for h, right in here:
+            to_mate(origin(s, right), y, h)
+        for h, right in here:
+            widen(origin(s, right), y, h, c, hr)
+        collect(s - 2)
+        collect_relayed(s - 4)
         if work:
             work.popleft()()
-        collect(s - 2)
     while work:
         work.popleft()()
     collect(half)
+    collect_relayed(half)
     whole = remote(table.at[:, :, c], table.at[:, :, 1 - c], psend.at[0], precv.at[0], mate)
     whole.wait_recv()
 
@@ -263,7 +313,7 @@
         e = v + res[a:b, :]
         df[...] = (e * lax.rsqrt(jnp.sum(e * e, axis=1, keepdims=True) + EPS)).astype(BF16)
         for which, docs in ((0, dc), (1, df)):
-            row = pl.multiple_of(which * 64 + x * PP, PP)
+            row = pl.multiple_of(fine0 if which else coarse0, PP)
             for n in range(nq // blk):
                 sim = lax.dot_general(docs[...], qn[n * blk:(n + 1) * blk, :], NT,
                                       preferred_element_type=F32)
@@ -275,14 +325,48 @@
     st[...] = lax.dot_general(ones, mp[...], NT, precision=lax.Precision.HIGHEST,
                               preferred_element_type=F32)
 
+    wide_lane, wide_row = iota(st.shape, 1), iota(st.shape, 0)
+    v = jnp.where(keep[...] == 1, st[...], LOW)
+    v = jnp.take_along_axis(v, fine0 + jnp.bitwise_and(wide_lane, PP - 1), axis=1,
+                            mode="promise_in_bounds")
+    v = jnp.where(wide_lane // 16 == jnp.bitwise_and(wide_row, 7), v, 0.0)
+    v = jnp.sum(v.reshape(2 * X, 8, 128), axis=1)
+    for k in range(X):
+        c1[k] = v[2 * k:2 * k + 2, :]
+
+    def layer(ox, oc):
+        i = ox * YC + oc
+        return remote(c1.at[lax.rem(x + ox, X)], c1buf.at[i], asend.at[i], arecv.at[i],
+                      {"query": lax.rem(x + ox, X), "cent": lax.rem(yc + oc, YC)})
+
+    layers = [(ox, oc) for ox in range(X) for oc in range(YC) if ox or oc]
+    layers.sort(key=lambda t: -min(t[0], X - t[0]) - min(t[1] // 2, Y - t[1] // 2))
+    for t in layers:
+        layer(*t).start()
     scopies = []
     for o in range(1, X):
         dst = pl.multiple_of(lax.rem(x + o, X) * 16, 16)
         scopies.append(remote(st.at[pl.ds(dst, 16)], sbuf.at[o - 1], ssend.at[o - 1],
                               srecv.at[o - 1], xpeer[o - 1]))
         scopies[-1].start()
-
-    lane = iota((16, 128), 1)
+    for t in layers:
+        layer(*t).wait()
+    row = iota((16, 128), 0)
+    at = 16 * jnp.bitwise_and(row, 7) + jnp.bitwise_and(lane, 15)
+    groups = [jnp.zeros((16, 128), F32) for _ in range(X * YC // 8)]
+    for i in range(X * YC):
+        v = c1buf[i] if i else c1[x]
+        v = jnp.concatenate([jnp.broadcast_to(v[0:1], (8, 128)),
+                             jnp.broadcast_to(v[1:2], (8, 128))], axis=0)
+        v = jnp.take_along_axis(v, at, axis=1, mode="promise_in_bounds")
+        groups[i // 8] = jnp.where(lane // 16 == i % 8, v, groups[i // 8])
+    first = (TOPK * iota((16, 1), 0)).astype(F32)
+    c2[...] = jnp.sum(top8(groups, first), axis=0, keepdims=True)
+    bcopies = []
+    for o in range(1, Z):
+        bcopies.append(remote(c2, c2buf.at[o - 1], bsend.at[o - 1], brecv.at[o - 1], zpeer[o - 1]))
+        bcopies[-1].start()
+
     rep = jnp.where(jnp.bitwise_and(lane, 15) == iota((16, 128), 0), 1.0, 0.0).astype(BF16)
     pos_t = jnp.dot(pos[...].astype(F32).astype(BF16), rep, preferred_element_type=F32).astype(I32)
     count = jnp.sum(jnp.where(iota((16, 16), 0) == iota((16, 16), 1), tally[...], 0),
@@ -293,24 +377,9 @@
     tot = st[pl.ds(pl.multiple_of(x * 16, 16), 16), :]
     for o in range(X - 1):
         tot = tot + sbuf[o]
-    fine = jnp.take_along_axis(tot, pos_t + 64, axis=1, mode="promise_in_bounds")
-    c1[...] = jnp.where(lane // 16 == yc, jnp.where(live, fine, LOW), 0.0)
-    acopies = []
-    for o in range(1, YC):
-        acopies.append(remote(c1, c1buf.at[o - 1], asend.at[o - 1], arecv.at[o - 1], cpeer[o - 1]))
-        acopies[-1].start()
-    coarse = jnp.take_along_axis(tot, pos_t, axis=1, mode="promise_in_bounds")
-    scores = jnp.where(live, jnp.where(lane < 16, coarse, fine), 0.0)
-    for cp in acopies:
-        cp.wait()
-    v = c1[...]
-    for o in range(YC - 1):
-        v = v + c1buf[o]
-    c2[...] = top8(v, z * TOPK)
-    bcopies = []
-    for o in range(1, Z):
-        bcopies.append(remote(c2, c2buf.at[o - 1], bsend.at[o - 1], brecv.at[o - 1], zpeer[o - 1]))
-        bcopies[-1].start()
+    where = pos_t + jnp.where(lane < 16, 64 * (1 - c), 64 * c)
+    slots = jnp.take_along_axis(tot, where, axis=1, mode="promise_in_bounds")
+    slots = jnp.where(live, slots, 0.0)
     for d in sent:
         d.wait_send()
     for o in range(1, Y):
@@ -319,10 +388,13 @@
     whole.wait_send()
     for cp in bcopies:
         cp.wait()
-    v = c2[...]
-    for o in range(Z - 1):
-        v = v + c2buf[o]
-    out[...] = jnp.where(lane < 32, scores, top8(v, 32))
+    at = TOPK * row + jnp.bitwise_and(lane, TOPK - 1)
+    merged = jnp.zeros((16, 128), F32)
+    for i in range(Z):
+        v = jnp.broadcast_to(c2buf[i - 1] if i else c2[...], (16, 128))
+        v = jnp.take_along_axis(v, at, axis=1, mode="promise_in_bounds")
+        merged = jnp.where(lane // TOPK == i, v, merged)
+    out[...] = jnp.where(lane < 32, slots, top8([merged], 32.0))
 
 
 def fused(X, Z, YC, means, queries, shard, entry, words, amounts, pos, tally):
@@ -351,14 +423,15 @@
             VMEM((X - 1, R, 128), BF16), VMEM((X - 1, R, 128), BF16),
             VMEM((CR, 128), BF16), VMEM((CR, 128), BF16),
             VMEM((128, nq), F32), VMEM((nq // 32, 128), F32), VMEM((X - 1, 16, 128), F32),
-            VMEM((16, 128), F32), VMEM((YC - 1, 16, 128), F32),
-            VMEM((16, 128), F32), VMEM((Z - 1, 16, 128), F32),
+            VMEM((X, 16, 16), I32), VMEM((X, 1, 16), I32), VMEM((nq // 32, 128), I32),
+            VMEM((X, 2, 128), F32), VMEM((X * YC, 2, 128), F32),
+            VMEM((1, 128), F32), VMEM((Z - 1, 1, 128), F32),
             dma((5 + X,)),
             dma((2, half)), dma((2, half)), dma((2, half)), dma((2, half)),
             dma((Y - 1,)), dma((2, 2 * half + 1, Y - 1)),
-            dma((X - 1,)), dma((X - 1,)), dma((1,)), dma((1,)),
+            dma((X - 1,)), dma((X - 1,)), dma((1,)), dma((1,)), dma((2, X - 1)), dma((2, X - 1)),
             dma((X - 1, CHUNKS)), dma((X - 1, CHUNKS)), dma((X - 1,)), dma((X - 1,)),
-            dma((YC - 1,)), dma((YC - 1,)), dma((Z - 1,)), dma((Z - 1,)),
+            dma((X * YC,)), dma((X * YC,)), dma((Z - 1,)), dma((Z - 1,)),
         ],
         compiler_params=pltpu.CompilerParams(
             collective_id=0, has_side_effects=True, vmem_limit_bytes=60 << 20),
@@ -370,10 +443,11 @@
           quantized_error_words, quantized_error_amounts, keeper_document_position,
           active_keeper_tally):
     X, Z, YC = (lax.axis_size(a) for a in ("query", "corpus", "cent"))
-    out = fused(X, Z, YC, cluster_means, request_term_embeds.reshape(-1, 128),
-                cluster_shard_number[:, :, 0], cluster_entry_within, quantized_error_words,
-                quantized_error_amounts, keeper_document_position[:, 0, :],
-                active_keeper_tally.reshape(1, 16))
+    out = fused(
+        X, Z, YC, cluster_means, request_term_embeds.reshape(-1, 128),
+        cluster_shard_number[:, :, 0], cluster_entry_within, quantized_error_words,
+        quantized_error_amounts, keeper_document_position[:, 0, :],
+        active_keeper_tally.reshape(1, 16))
     return out[:, None, 0:16], out[:, None, 16:32], out[:, 32:32 + TOPK]
 
 

time: 83.2 us -> 75.8 us (0.911)
  Pallas kernels: 80.2 us -> 72.7 us
    pallas_call x1, Pallas kernels: 80.2 us -> 72.7 us  [fused(): pl.pallas_call(functools.partial(kernel, X, Z, Y), out_shape=jax.ShapeDty...]
where the time goes in v3:
time: 75.8 us; the launch traced here: 75.5 us
  Pallas kernels  72.7 us (96%)
  local copies, waits for them, and re-layouts  2.14 us (3%)
    pallas_call x1, Pallas kernels, fused(): pl.pallas_call(functools.partial(kernel, X, Z, Y), out_shape=jax.ShapeDty...  72.7 us

profile of v3, /device:TPU:1, one launch (start us, length us, event | category | flops | bytes accessed | tf_op | source)
XLA Modules:
  0.0 75.5 jit_solution(16656710225209821603)
XLA Ops:
  0.6 72.7 %plaid.1 = f32[16,128]{1,0:T(8,128)} custom-call(bf16[512,128]{1,0:T(8,128)(2,1)} %means.1, bf16[512,128]{1,0:T(8,128)(2,1)} %bitcast.10, s32[64,64]{1,0:T(8,128)} %bitcast.11, s32[64,64]{1,0:T(8,128)} %entry.1, s32[64,1024]{1,0:T(8,128)} %words.1, f32[4]{0:T(128)} %amounts.1, s32[16,16]{1,0:T(8,128)} %bitcast.12, s32[1,16]{1,0:T(1,128)} %bitcast.15), custom_call_target="tpu_custom_call" | custom-call | tf_op jit(solution)/shard_map/plaid/pallas_call | solution.py:412
  73.4 0.8 %slice.11 = f32[16,8]{1,0:T(8,128)S(1)} slice(f32[16,128]{1,0:T(8,128)} %plaid.1), slice={[0:16], [32:40]} | slice | bytes 1024 | tf_op jit(solution)/shard_map/slice | solution.py:451
  74.1 0.0 copy-start
  74.1 0.7 copy.13
  74.8 0.0 copy-done
  74.8 0.7 fusion
Async XLA Ops:
  74.1 0.7 copy-start

commit v4 on v3

--- a/solution.py
+++ b/solution.py
@@ -17,7 +17,7 @@
 I32 = jnp.int32
 VMEM = pltpu.VMEM
 NT = (((1,), (1,)), ((), ()))
-CHUNKS = 4
+CHUNKS = 8
 
 
 def iota(shape, axis):
@@ -253,8 +253,8 @@
             to_mate(origin(s, right), y, h)
         for h, right in here:
             widen(origin(s, right), y, h, c, hr)
-        collect(s - 2)
-        collect_relayed(s - 4)
+        collect(s - 3)
+        collect_relayed(s - 5)
         if work:
             work.popleft()()
     while work:

time: 75.8 us -> 75.4 us (level)
  no operation moved by 1% of the time
where the time goes in v4:
time: 75.4 us; the launch traced here: 75.2 us
  Pallas kernels  72.4 us (96%)
  local copies, waits for them, and re-layouts  2.14 us (3%)
    pallas_call x1, Pallas kernels, fused(): pl.pallas_call(functools.partial(kernel, X, Z, Y), out_shape=jax.ShapeDty...  72.4 us

profile of v4, /device:TPU:1, one launch (start us, length us, event | category | flops | bytes accessed | tf_op | source)
XLA Modules:
  0.0 75.2 jit_solution(10032270731568102904)
XLA Ops:
  0.6 72.4 %plaid.1 = f32[16,128]{1,0:T(8,128)} custom-call(bf16[512,128]{1,0:T(8,128)(2,1)} %means.1, bf16[512,128]{1,0:T(8,128)(2,1)} %bitcast.10, s32[64,64]{1,0:T(8,128)} %bitcast.11, s32[64,64]{1,0:T(8,128)} %entry.1, s32[64,1024]{1,0:T(8,128)} %words.1, f32[4]{0:T(128)} %amounts.1, s32[16,16]{1,0:T(8,128)} %bitcast.12, s32[1,16]{1,0:T(1,128)} %bitcast.15), custom_call_target="tpu_custom_call" | custom-call | tf_op jit(solution)/shard_map/plaid/pallas_call | solution.py:412
  73.0 0.8 %slice.11 = f32[16,8]{1,0:T(8,128)S(1)} slice(f32[16,128]{1,0:T(8,128)} %plaid.1), slice={[0:16], [32:40]} | slice | bytes 1024 | tf_op jit(solution)/shard_map/slice | solution.py:451
  73.8 0.0 copy-start
  73.8 0.7 copy.13
  74.5 0.0 copy-done
  74.5 0.7 fusion
Async XLA Ops:
  73.8 0.7 copy-start
